TPU v7x, 256 devices: a whole 4x4x8 slice. The times are simulated.
256 devices in a mesh: ctx: 128 (over z, y_lo, x, core), head: 2 (over y_hi).
Axes of the slice: x: 4, y: 4 (y_hi: 2, y_lo: 2; y = y_hi * 2 + y_lo), z: 8, core: 2. Of those that a mesh axis runs over, the one named last changes fastest.
Arguments:
- queries: bfloat16 [49152, 2048], P('ctx', 'head')
- keys: bfloat16 [49152, 512], P('ctx', 'head')
- values: bfloat16 [49152, 512], P('ctx', 'head'), may hold values from -6 to 6
- block_start: int32 [384], P('ctx'), may hold values from 0 to 49024, as said below
- out_weight: bfloat16 [2048, 4096], P('head'), may hold values from -0.125 to 0.125
Outputs:
- attended: bfloat16 [49152, 4096], P('ctx', 'head')
Inputs may be any that keep to these rules, and one draw needn't show every extreme that they name: block_start never falls; every document is a whole number of blocks and at most 3072 tokens long, and one document is exactly 3072 tokens long; the first and the last block each begin a document.
All inputs are finite; a program needn't handle non-finite values.
Results may differ from a plain program's by a relative error of at most 0.012.
Values may be sent and summed in bfloat16 or wider, within the bound.
A program may use at most 64 MiB of HBM per device.

v0:
```python
import jax
import jax.numpy as jnp
from jax import lax
from jax.sharding import PartitionSpec as P

HEAD_SIZE = 128
BLOCK = 128
SPAN = 8


def from_behind(block, axis, distance):
    devices = range(lax.axis_size(axis))
    route = [(i - distance, i) for i in devices if i - distance in devices]
    return lax.ppermute(block, axis, route)


def per_device(queries, keys, values, block_start, out_weight):
    tok = queries.shape[0]
    kv_heads = keys.shape[1] // HEAD_SIZE
    q_heads = queries.shape[1] // HEAD_SIZE
    query_group = q_heads // kv_heads
    scale = HEAD_SIZE ** (-0.5)
    first_token = lax.axis_index("ctx") * tok
    q_pos = first_token + jnp.arange(tok, dtype=jnp.int32)
    starts = jnp.repeat(block_start, BLOCK)
    lowest = jnp.min(starts)
    query_rows = queries.reshape(tok, kv_heads, query_group, HEAD_SIZE)
    packed = jnp.stack([keys, values])

    def attend(state, pair, key_first):
        top, total, accum = state
        key_blk = pair[0].reshape(tok, kv_heads, HEAD_SIZE)
        val_blk = pair[1].reshape(tok, kv_heads, HEAD_SIZE)
        scores = (
            jnp.einsum("pgcd,jgd->gcpj", query_rows, key_blk, preferred_element_type=jnp.float32)
            * scale
        )
        k_pos = key_first + jnp.arange(tok, dtype=jnp.int32)
        valid = (k_pos[None, :] >= starts[:, None]) & (k_pos[None, :] <= q_pos[:, None])
        masked = jnp.where(valid, scores, -1e30)
        top_new = jnp.maximum(top, jnp.max(masked, axis=-1))
        factor = jnp.exp(top - top_new)
        expw = jnp.where(valid, jnp.exp(masked - top_new[..., None]), 0.0)
        total = total * factor + jnp.sum(expw, axis=-1)
        update = jnp.einsum(
            "gcpj,jgd->gcpd", expw.astype(jnp.bfloat16), val_blk, preferred_element_type=jnp.float32
        )
        accum = accum * factor[..., None] + update
        return (top_new, total, accum)

    state = (
        jnp.full((kv_heads, query_group, tok), -1e30, jnp.float32),
        jnp.zeros((kv_heads, query_group, tok), jnp.float32),
        jnp.zeros((kv_heads, query_group, tok, HEAD_SIZE), jnp.float32),
    )
    state = attend(state, packed, first_token)
    moving = packed
    for step in range(1, SPAN + 1):
        moving = from_behind(moving, "ctx", 1)
        maybe_pair = moving
        maybe_key_first = first_token - step * tok
        needed = lowest <= maybe_key_first + tok - 1
        state = lax.cond(
            needed, lambda s: attend(s, maybe_pair, maybe_key_first), lambda s: s, state
        )
    top, total, accum = state
    heads_out = (accum / total[..., None]).astype(jnp.bfloat16)
    heads_out = jnp.transpose(heads_out, (2, 0, 1, 3)).reshape(tok, q_heads * HEAD_SIZE)
    summed = lax.psum_scatter(
        lax.dot_general(
            out_weight, heads_out, (((0,), (1,)), ((), ())), preferred_element_type=jnp.float32
        ).astype(jnp.bfloat16),
        "head",
        scatter_dimension=0,
        tiled=True,
    ).astype(jnp.float32)
    return summed.T.astype(jnp.bfloat16)


def solution(mesh):
    in_specs = (P("ctx", "head"), P("ctx", "head"), P("ctx", "head"), P("ctx"), P("head", None))
    out_specs = P("ctx", "head")
    return jax.shard_map(
        per_device, mesh=mesh, in_specs=in_specs, out_specs=out_specs, check_vma=False
    )
```

profile of v0, /device:TPU:1, one launch (start us, length us, event | category | flops | bytes accessed | tf_op | source)
XLA Modules:
  0.0 199.9 jit_solution(12910939636367152854)
XLA Ops:
  6.5 1.1 copy.46
  7.6 1.1 copy.47
  8.8 4.5 %collective-permute-start = (bf16[2,384,256]{1,2,0:T(8,128)(2,1)S(1)}, bf16[2,384,256]{1,2,0:T(8,128)(2,1)S(1)}, u32[]{:S(2)}, u32[]{:S(2)}) collective-permute-start(bf16[2,384,256]{1,2,0:T(8,128)(2,1)S(1)} %pad_maximum_fusion), channel_id=1, source_target_pairs={{0,2},{2,4},{4,6},{6,8},{8,10},{10,12},{12,14},{14,16},{16,18},{18... | collective-permute-start | bytes 1179656 | tf_op jit(solution)/shard_map/ppermute | solution.py:14
  13.3 4.7 %collective-permute-done = bf16[2,384,256]{1,2,0:T(8,128)(2,1)S(1)} collective-permute-done((bf16[2,384,256]{1,2,0:T(8,128)(2,1)S(1)}, bf16[2,384,256]{1,2,0:T(8,128)(2,1)S(1)}, u32[]{:S(2)}, u32[]{:S(2)}) %collective-permute-start) | collective-permute-done | bytes 393248 | tf_op jit(solution)/shard_map/ppermute | solution.py:14
  18.0 4.4 %collective-permute-start.1 = (bf16[2,384,256]{1,2,0:T(8,128)(2,1)S(1)}, bf16[2,384,256]{1,2,0:T(8,128)(2,1)S(1)}, u32[]{:S(2)}, u32[]{:S(2)}) collective-permute-start(bf16[2,384,256]{1,2,0:T(8,128)(2,1)S(1)} %collective-permute-done), channel_id=1, source_target_pairs={{0,2},{2,4},{4,6},{6,8},{8,10},{10,12},{12,14},{14,16},{16,18},{18... | collective-permute-start | bytes 1179656 | tf_op jit(solution)/shard_map/ppermute | solution.py:14
  22.4 4.7 %collective-permute-done.1 = bf16[2,384,256]{1,2,0:T(8,128)(2,1)S(1)} collective-permute-done((bf16[2,384,256]{1,2,0:T(8,128)(2,1)S(1)}, bf16[2,384,256]{1,2,0:T(8,128)(2,1)S(1)}, u32[]{:S(2)}, u32[]{:S(2)}) %collective-permute-start.1) | collective-permute-done | bytes 393248 | tf_op jit(solution)/shard_map/ppermute | solution.py:14
  27.1 4.4 %collective-permute-start.2 = (bf16[2,384,256]{1,2,0:T(8,128)(2,1)S(1)}, bf16[2,384,256]{1,2,0:T(8,128)(2,1)S(1)}, u32[]{:S(2)}, u32[]{:S(2)}) collective-permute-start(bf16[2,384,256]{1,2,0:T(8,128)(2,1)S(1)} %collective-permute-done.1), channel_id=1, source_target_pairs={{0,2},{2,4},{4,6},{6,8},{8,10},{10,12},{12,14},{14,16},{16,18},{18... | collective-permute-start | bytes 1179656 | tf_op jit(solution)/shard_map/ppermute | solution.py:14
  31.5 4.7 %collective-permute-done.2 = bf16[2,384,256]{1,2,0:T(8,128)(2,1)S(1)} collective-permute-done((bf16[2,384,256]{1,2,0:T(8,128)(2,1)S(1)}, bf16[2,384,256]{1,2,0:T(8,128)(2,1)S(1)}, u32[]{:S(2)}, u32[]{:S(2)}) %collective-permute-start.2) | collective-permute-done | bytes 393248 | tf_op jit(solution)/shard_map/ppermute | solution.py:14
  36.2 4.4 %collective-permute-start.3 = (bf16[2,384,256]{1,2,0:T(8,128)(2,1)S(1)}, bf16[2,384,256]{1,2,0:T(8,128)(2,1)S(1)}, u32[]{:S(2)}, u32[]{:S(2)}) collective-permute-start(bf16[2,384,256]{1,2,0:T(8,128)(2,1)S(1)} %collective-permute-done.2), channel_id=1, source_target_pairs={{0,2},{2,4},{4,6},{6,8},{8,10},{10,12},{12,14},{14,16},{16,18},{18... | collective-permute-start | bytes 1179656 | tf_op jit(solution)/shard_map/ppermute | solution.py:14
  40.5 4.7 %collective-permute-done.3 = bf16[2,384,256]{1,2,0:T(8,128)(2,1)S(1)} collective-permute-done((bf16[2,384,256]{1,2,0:T(8,128)(2,1)S(1)}, bf16[2,384,256]{1,2,0:T(8,128)(2,1)S(1)}, u32[]{:S(2)}, u32[]{:S(2)}) %collective-permute-start.3) | collective-permute-done | bytes 393248 | tf_op jit(solution)/shard_map/ppermute | solution.py:14
  45.3 4.4 %collective-permute-start.4 = (bf16[2,384,256]{1,2,0:T(8,128)(2,1)S(1)}, bf16[2,384,256]{1,2,0:T(8,128)(2,1)S(1)}, u32[]{:S(2)}, u32[]{:S(2)}) collective-permute-start(bf16[2,384,256]{1,2,0:T(8,128)(2,1)S(1)} %collective-permute-done.3), channel_id=1, source_target_pairs={{0,2},{2,4},{4,6},{6,8},{8,10},{10,12},{12,14},{14,16},{16,18},{18... | collective-permute-start | bytes 1179656 | tf_op jit(solution)/shard_map/ppermute | solution.py:14
  49.6 1.4 broadcast_bitcast_fusion
  52.0 1.5 copy.41
  54.3 4.4 %collective-permute-start.5 = (bf16[2,384,256]{1,2,0:T(8,128)(2,1)S(1)}, bf16[2,384,256]{1,2,0:T(8,128)(2,1)S(1)}, u32[]{:S(2)}, u32[]{:S(2)}) collective-permute-start(bf16[2,384,256]{1,2,0:T(8,128)(2,1)S(1)} %collective-permute-done.4), channel_id=1, source_target_pairs={{0,2},{2,4},{4,6},{6,8},{8,10},{10,12},{12,14},{14,16},{16,18},{18... | collective-permute-start | bytes 1179656 | tf_op jit(solution)/shard_map/ppermute | solution.py:14
  59.7 3.7 %collective-permute-done.5 = bf16[2,384,256]{1,2,0:T(8,128)(2,1)S(1)} collective-permute-done((bf16[2,384,256]{1,2,0:T(8,128)(2,1)S(1)}, bf16[2,384,256]{1,2,0:T(8,128)(2,1)S(1)}, u32[]{:S(2)}, u32[]{:S(2)}) %collective-permute-start.5) | collective-permute-done | bytes 393248 | tf_op jit(solution)/shard_map/ppermute | solution.py:14
  63.4 4.4 %collective-permute-start.6 = (bf16[2,384,256]{1,2,0:T(8,128)(2,1)S(1)}, bf16[2,384,256]{1,2,0:T(8,128)(2,1)}, u32[]{:S(2)}, u32[]{:S(2)}) collective-permute-start(bf16[2,384,256]{1,2,0:T(8,128)(2,1)S(1)} %collective-permute-done.5), channel_id=1, source_target_pairs={{0,2},{2,4},{4,6},{6,8},{8,10},{10,12},{12,14},{14,16},{16,18},{18... | collective-permute-start | bytes 1179656 | tf_op jit(solution)/shard_map/ppermute | solution.py:14
  67.8 1.2 fusion.91
  74.0 3.0 %collective-permute-start.7 = (bf16[2,384,256]{1,2,0:T(8,128)(2,1)}, bf16[2,384,256]{1,2,0:T(8,128)(2,1)S(1)}, u32[]{:S(2)}, u32[]{:S(2)}) collective-permute-start(bf16[2,384,256]{1,2,0:T(8,128)(2,1)} %collective-permute-done.6), channel_id=1, source_target_pairs={{0,2},{2,4},{4,6},{6,8},{8,10},{10,12},{12,14},{14,16},{16,18},{18... | collective-permute-start | bytes 1179656 | tf_op jit(solution)/shard_map/ppermute | solution.py:14
  77.0 3.6 %fusion.95 = f32[2,4,384,128]{3,2,1,0:T(8,128)S(1)} fusion(f32[2,384,384,4]{2,1,3,0:T(8,128)} %copy-done, f32[2,4,384]{2,1,0:T(4,128)S(1)} %broadcast_maximum_fusion, pred[384,384]{0,1:T(8,128)(4,1)S(1)} %compare_and_fusion.8, f32[2,4,384]{2,1,0:T(4,128)S(1)} %get-tuple-element.440, bf16[384,2,128,1]{2,1,0,3:T(2,128)(2,1)S(1)} %bitcast.345), kind=kOutput, calls=%fused_computation.130 | convolution fusion | flops 308281344 | bytes 6660096 | tf_op jit(solution)/shard_map/gcpj,jgd->gcpd/dot_general | solution.py:45
  80.7 5.5 %conditional.8 = ((f32[2,4,384]{2,1,0:T(4,128)S(1)}, f32[2,4,384]{2,1,0:T(4,128)S(1)}, f32[2,4,384,128]{3,2,1,0:T(8,128)S(1)})) conditional(s32[]{:T(128)} %convert_element_type.74, (f32[2,4,384]{2,1,0:T(4,128)S(1)}, f32[2,4,384]{2,1,0:T(4,128)S(1)}, f32[2,4,384,128]{3,2,1,0:T(8,128)S(1)}) %tuple.61, (s32[]{:T(128)}, s32[3,128]{1,0:T(4,128)S(1)}, ...), branch_computations={%region_3.4_spmd, %region_4.7_spmd} | conditional | flops 620550528 | bytes 20060196 | solution.py:63
  83.0 1.1 fusion.2
  84.1 2.0 %multiply_add_fusion = f32[2,4,384,128]{3,2,1,0:T(8,128)S(1)} fusion(f32[2,4,384,128]{3,2,1,0:T(8,128)S(1)} %get-tuple-element.222, bf16[384,2,128,1]{0,2,3,1:T(8,128)(2,1)S(1)} %bitcast.346, f32[2,384,384,4]{2,1,3,0:T(8,128)S(1)} %get-tuple-element.411, f32[2,4,384]{2,1,0:T(4,128)S(1)} %max.18, pred[384,384]{0,1:T(8,128)(4,1)S(1)} %compare_and_fusion, ...), kind=kOutput, calls=%fused_computation.7 | convolution fusion | flops 308674560 | bytes 8232960 | tf_op jit(solution)/shard_map/cond/branch_1_fun/gcpj,jgd->gcpd/dot_general | solution.py:45
  89.1 8.5 %fusion.88 = bf16[4096,384]{0,1:T(8,128)(2,1)} fusion(bf16[384,1024]{0,1:T(8,128)(2,1)S(1)} %bitcast.337, bf16[1024,4096]{1,0:T(8,128)(2,1)} %param.25), kind=kOutput, calls=%fused_computation.121 | convolution fusion | flops 3222798336 | bytes 12320768 | tf_op jit(solution)/shard_map/dot_general | solution.py:70
  97.6 95.4 %reduce-scatter.2.cloned.1.call-done = bf16[2048,384]{0,1:T(8,128)(2,1)} async-done(((bf16[4096,384]{0,1:T(8,128)(2,1)}), bf16[2048,384]{0,1:T(8,128)(2,1)}) %reduce-scatter.2.cloned.1.call-update) | async-done | bytes 1572880 | tf_op jit(solution)/shard_map/reduce_scatter | solution.py:69
  (54 shorter events, 8.5 us)
Async XLA Ops:
  6.5 186.5 %reduce-scatter.2.cloned.1.call-start = ((), (), s32[]{:S(2)}) async-start(), calls=%async_computation.1 | async-start | bytes 4718592 | tf_op jit(solution)/shard_map/reduce_scatter | solution.py:69
  8.8 9.2 %collective-permute-start = (bf16[2,384,256]{1,2,0:T(8,128)(2,1)S(1)}, bf16[2,384,256]{1,2,0:T(8,128)(2,1)S(1)}, u32[]{:S(2)}, u32[]{:S(2)}) collective-permute-start(bf16[2,384,256]{1,2,0:T(8,128)(2,1)S(1)} %pad_maximum_fusion), channel_id=1, source_target_pairs={{0,2},{2,4},{4,6},{6,8},{8,10},{10,12},{12,14},{14,16},{16,18},{18... | collective-permute-start | bytes 1179656 | tf_op jit(solution)/shard_map/ppermute | solution.py:14
  18.0 4.4 %copy-start.10 = (bf16[2,384,256]{1,2,0:T(8,128)(2,1)}, bf16[2,384,256]{1,2,0:T(8,128)(2,1)S(1)}, u32[]{:S(2)}) copy-start(bf16[2,384,256]{1,2,0:T(8,128)(2,1)S(1)} %collective-permute-done) | copy-start | bytes 1179652
  18.0 9.1 %collective-permute-start.1 = (bf16[2,384,256]{1,2,0:T(8,128)(2,1)S(1)}, bf16[2,384,256]{1,2,0:T(8,128)(2,1)S(1)}, u32[]{:S(2)}, u32[]{:S(2)}) collective-permute-start(bf16[2,384,256]{1,2,0:T(8,128)(2,1)S(1)} %collective-permute-done), channel_id=1, source_target_pairs={{0,2},{2,4},{4,6},{6,8},{8,10},{10,12},{12,14},{14,16},{16,18},{18... | collective-permute-start | bytes 1179656 | tf_op jit(solution)/shard_map/ppermute | solution.py:14
  27.1 18.2 %copy-start.8 = (bf16[2,384,256]{1,2,0:T(8,128)(2,1)}, bf16[2,384,256]{1,2,0:T(8,128)(2,1)S(1)}, u32[]{:S(2)}) copy-start(bf16[2,384,256]{1,2,0:T(8,128)(2,1)S(1)} %collective-permute-done.1) | copy-start | bytes 1179652
  27.1 9.1 %collective-permute-start.2 = (bf16[2,384,256]{1,2,0:T(8,128)(2,1)S(1)}, bf16[2,384,256]{1,2,0:T(8,128)(2,1)S(1)}, u32[]{:S(2)}, u32[]{:S(2)}) collective-permute-start(bf16[2,384,256]{1,2,0:T(8,128)(2,1)S(1)} %collective-permute-done.1), channel_id=1, source_target_pairs={{0,2},{2,4},{4,6},{6,8},{8,10},{10,12},{12,14},{14,16},{16,18},{18... | collective-permute-start | bytes 1179656 | tf_op jit(solution)/shard_map/ppermute | solution.py:14
  36.2 9.1 %copy-start.7 = (bf16[2,384,256]{1,2,0:T(8,128)(2,1)}, bf16[2,384,256]{1,2,0:T(8,128)(2,1)S(1)}, u32[]{:S(2)}) copy-start(bf16[2,384,256]{1,2,0:T(8,128)(2,1)S(1)} %collective-permute-done.2) | copy-start | bytes 1179652
  36.2 9.1 %collective-permute-start.3 = (bf16[2,384,256]{1,2,0:T(8,128)(2,1)S(1)}, bf16[2,384,256]{1,2,0:T(8,128)(2,1)S(1)}, u32[]{:S(2)}, u32[]{:S(2)}) collective-permute-start(bf16[2,384,256]{1,2,0:T(8,128)(2,1)S(1)} %collective-permute-done.2), channel_id=1, source_target_pairs={{0,2},{2,4},{4,6},{6,8},{8,10},{10,12},{12,14},{14,16},{16,18},{18... | collective-permute-start | bytes 1179656 | tf_op jit(solution)/shard_map/ppermute | solution.py:14
  45.2 8.5 %copy-start.5 = (bf16[2,384,256]{1,2,0:T(8,128)(2,1)}, bf16[2,384,256]{1,2,0:T(8,128)(2,1)S(1)}, u32[]{:S(2)}) copy-start(bf16[2,384,256]{1,2,0:T(8,128)(2,1)S(1)} %collective-permute-done.3) | copy-start | bytes 1179652
  45.3 9.1 %collective-permute-start.4 = (bf16[2,384,256]{1,2,0:T(8,128)(2,1)S(1)}, bf16[2,384,256]{1,2,0:T(8,128)(2,1)S(1)}, u32[]{:S(2)}, u32[]{:S(2)}) collective-permute-start(bf16[2,384,256]{1,2,0:T(8,128)(2,1)S(1)} %collective-permute-done.3), channel_id=1, source_target_pairs={{0,2},{2,4},{4,6},{6,8},{8,10},{10,12},{12,14},{14,16},{16,18},{18... | collective-permute-start | bytes 1179656 | tf_op jit(solution)/shard_map/ppermute | solution.py:14
  54.3 22.7 %copy-start.4 = (bf16[2,384,256]{1,2,0:T(8,128)(2,1)}, bf16[2,384,256]{1,2,0:T(8,128)(2,1)S(1)}, u32[]{:S(2)}) copy-start(bf16[2,384,256]{1,2,0:T(8,128)(2,1)S(1)} %collective-permute-done.4) | copy-start | bytes 1179652
  54.3 9.1 %collective-permute-start.5 = (bf16[2,384,256]{1,2,0:T(8,128)(2,1)S(1)}, bf16[2,384,256]{1,2,0:T(8,128)(2,1)S(1)}, u32[]{:S(2)}, u32[]{:S(2)}) collective-permute-start(bf16[2,384,256]{1,2,0:T(8,128)(2,1)S(1)} %collective-permute-done.4), channel_id=1, source_target_pairs={{0,2},{2,4},{4,6},{6,8},{8,10},{10,12},{12,14},{14,16},{16,18},{18... | collective-permute-start | bytes 1179656 | tf_op jit(solution)/shard_map/ppermute | solution.py:14
  58.7 10.3 %copy-start.1 = (bf16[384,256]{1,0:T(8,128)(2,1)S(1)}, bf16[384,256]{1,0:T(8,128)(2,1)}, u32[]{:S(2)}) copy-start(bf16[384,256]{1,0:T(8,128)(2,1)} %param.23) | copy-start | bytes 589828
  59.7 8.1 %copy-start = (f32[2,384,384,4]{2,1,3,0:T(8,128)}, f32[2,384,384,4]{2,1,3,0:T(8,128)S(1)}, u32[]{:S(2)}) copy-start(f32[2,384,384,4]{2,1,3,0:T(8,128)S(1)} %get-tuple-element.445) | copy-start | bytes 14155780
  63.4 13.6 %copy-start.2 = (bf16[2,384,256]{1,2,0:T(8,128)(2,1)}, bf16[2,384,256]{1,2,0:T(8,128)(2,1)S(1)}, u32[]{:S(2)}) copy-start(bf16[2,384,256]{1,2,0:T(8,128)(2,1)S(1)} %collective-permute-done.5) | copy-start | bytes 1179652
  63.4 10.5 %collective-permute-start.6 = (bf16[2,384,256]{1,2,0:T(8,128)(2,1)S(1)}, bf16[2,384,256]{1,2,0:T(8,128)(2,1)}, u32[]{:S(2)}, u32[]{:S(2)}) collective-permute-start(bf16[2,384,256]{1,2,0:T(8,128)(2,1)S(1)} %collective-permute-done.5), channel_id=1, source_target_pairs={{0,2},{2,4},{4,6},{6,8},{8,10},{10,12},{12,14},{14,16},{16,18},{18... | collective-permute-start | bytes 1179656 | tf_op jit(solution)/shard_map/ppermute | solution.py:14
  74.0 14.2 %collective-permute-start.7 = (bf16[2,384,256]{1,2,0:T(8,128)(2,1)}, bf16[2,384,256]{1,2,0:T(8,128)(2,1)S(1)}, u32[]{:S(2)}, u32[]{:S(2)}) collective-permute-start(bf16[2,384,256]{1,2,0:T(8,128)(2,1)} %collective-permute-done.6), channel_id=1, source_target_pairs={{0,2},{2,4},{4,6},{6,8},{8,10},{10,12},{12,14},{14,16},{16,18},{18... | collective-permute-start | bytes 1179656 | tf_op jit(solution)/shard_map/ppermute | solution.py:14
  77.0 3.6 %copy-start.11 = (s32[3]{0:T(128)S(1)}, s32[3]{0:T(128)}, u32[]{:S(2)}) copy-start(s32[3]{0:T(128)} %param.24) | copy-start | bytes 40
  80.7 5.5 %copy-start.9 = (bf16[2,384,256]{1,2,0:T(8,128)(2,1)S(1)}, bf16[2,384,256]{1,2,0:T(8,128)(2,1)}, u32[]{:S(2)}) copy-start(bf16[2,384,256]{1,2,0:T(8,128)(2,1)} %copy-done.8) | copy-start | bytes 1179652
  86.2 1.0 copy-start.6
  87.2 1.0 copy-start.3
Sparse Core Ops, SparseCore 0:
  97.8 95.2 reduce-scatter.1
where the time goes:
time: 201 us; the launch traced here: 200 us
  waiting for transfers between devices  119 us (59%)
  starting transfers between devices  33.8 us (17%)
  between operations  18.6 us (9%)
  matrix products  16 us (8%)
  local copies, waits for them, and re-layouts  8.13 us (4%)
  other arithmetic  4.3 us (2%)
    reduce_scatter x1, waiting for transfers between devices, per_device(): lax.psum_scatter(lax.dot_general(out_weight, heads_out, (((0,), (1,)), ((...  95.4 us
    ppermute x8, starting transfers between devices, from_behind(): return lax.ppermute(block, axis, route)  33.8 us
    ppermute x8, waiting for transfers between devices, from_behind(): return lax.ppermute(block, axis, route)  23.1 us
    dot_general x1, matrix products, per_device(): lax.dot_general(out_weight, heads_out, (((0,), (1,)), ((), ())), preferre...  8.5 us
    dot_general x2, matrix products, attend(): jnp.einsum('gcpj,jgd->gcpd', expw.astype(jnp.bfloat16), val_blk, preferre...  5.62 us
    unnamed x27, local copies, waits for them, and re-layouts  5.5 us
  transfers between devices with their start and end apart: 9, of which 7 were waited for; matrix products, arithmetic and copies ran while one was open for 8% of the time, Pallas kernels for 0%

commit v1 on v0

v1 whole, which is shorter than its diff:
```python
import math

import jax
import jax.numpy as jnp
from jax import lax
from jax.experimental import pallas as pl
from jax.experimental.pallas import tpu as pltpu
from jax.sharding import PartitionSpec as P

HEAD_SIZE = 128
BLOCK = 128
SPAN = 8
NX = 4
NY = 2
ROW = NX * 2
PLANE = NY * ROW
MESH = pl.DeviceIdType.MESH
MASKED = -1e30


def span_of(n, size):
    start = n * size
    return pl.ds(start if isinstance(start, int) else pl.multiple_of(start, size), size)


def kernel(
    starts,
    q_hbm,
    k_hbm,
    v_hbm,
    w_hbm,
    o_hbm,
    qb,
    kb,
    vb,
    sb,
    pb,
    bias,
    ho,
    hin,
    relay,
    wown,
    wfar,
    acc,
    outb,
    loc_sem,
    kv_send,
    kv_recv,
    w_send,
    w_recv,
    h_send,
    h_recv,
    f_send,
    f_recv,
    out_sem,
):
    n_ctx = lax.axis_size("ctx")
    tok = q_hbm.shape[0]
    kv_heads = k_hbm.shape[1] // HEAD_SIZE
    q_heads = q_hbm.shape[1] // HEAD_SIZE
    group = q_heads // kv_heads
    half = outb.shape[1]
    nz = n_ctx // PLANE
    piece = wfar.shape[0] // (nz * 2)
    up_hops = (nz - 1) // 2
    down_hops = nz - 1 - up_hops
    blocks = tok // BLOCK
    first = BLOCK
    keys = SPAN * tok + tok - first

    i = lax.axis_index("ctx")
    h = lax.axis_index("head")
    k = i % 2
    x = (i // 2) % NX
    y_lo = (i // ROW) % NY
    z = i // PLANE
    row0 = i - x * 2

    def dev(c, g):
        return {"ctx": c, "head": g}

    sib = dev(i + 1 - 2 * k, h)
    x_up = dev(row0 + ((x + 1) % NX) * 2, h)
    x_dn = dev(row0 + ((x + NX - 1) % NX) * 2, h)
    nxt = dev((i + ROW) % n_ctx, h)
    prv = dev((i + n_ctx - ROW) % n_ctx, h)
    yx = i + ROW - 2 * ROW * y_lo
    y_same = dev(yx, h)
    y_far = dev(yx, 1 - h)
    z_up = dev((i + PLANE) % n_ctx, h)
    z_dn = dev((i + n_ctx - PLANE) % n_ctx, h)

    local = []

    def load(src, dst):
        c = pltpu.make_async_copy(src, dst, loc_sem.at[len(local)])
        c.start()
        local.append(c)
        return c

    own = pl.ds(SPAN * tok, tok)
    kv_local = []
    for g in range(kv_heads):
        cols = pl.ds(g * HEAD_SIZE, HEAD_SIZE)
        kv_local.append(load(k_hbm.at[:, cols], kb.at[g, own, :]))
        kv_local.append(load(v_hbm.at[:, cols], vb.at[g, own, pl.ds(0, HEAD_SIZE)]))
    q_local = [load(q_hbm.at[:, pl.ds(n * HEAD_SIZE, HEAD_SIZE)], qb.at[n]) for n in range(q_heads)]
    w_local = load(w_hbm.at[:, span_of(h, half)], wown)

    barrier = pltpu.get_barrier_semaphore()
    partners = (sib, x_up, x_dn, nxt, prv, y_far, z_up, z_dn)
    for d in partners:
        pl.semaphore_signal(barrier, inc=1, device_id=d, device_id_type=MESH)
    pl.semaphore_wait(barrier, len(partners))

    def w_rows(p):
        return span_of(p, piece)

    def w_copy(p, slot, target):
        return pltpu.make_async_remote_copy(
            src_ref=wfar.at[w_rows(p), :],
            dst_ref=wfar.at[w_rows(p), :],
            send_sem=w_send.at[slot],
            recv_sem=w_recv.at[p],
            device_id=target,
            device_id_type=MESH,
        )

    mine = z * 2 + k
    w_first = pltpu.make_async_remote_copy(
        src_ref=w_hbm.at[w_rows(mine), span_of(1 - h, half)],
        dst_ref=wfar.at[w_rows(mine), :],
        send_sem=w_send.at[0],
        recv_sem=w_recv.at[mine],
        device_id=y_far,
        device_id_type=MESH,
    )
    w_first.start()

    w_plan = {0: [(mine, [(1, z_up), (2, z_dn), (3, sib)])]}
    slots = 4
    for d in range(1, down_hops + 1):
        w_plan[d] = []
        for reach, source, onward in (
            (up_hops, (z + nz - d) % nz, z_up),
            (down_hops, (z + d) % nz, z_dn),
        ):
            if d <= reach:
                targets = [onward, sib] if d < reach else [sib]
                w_plan[d].append((source * 2 + k, [(slots + n, c) for n, c in enumerate(targets)]))
                slots += len(targets)

    def w_step(d):
        for p, sends in w_plan[d]:
            w_copy(p, 0, sib).wait_recv()
            for slot, target in sends:
                w_copy(p, slot, target).start()

    def w_rest():
        for other in range(nz):
            w_copy(other * 2 + 1 - k, 0, sib).wait_recv()

    def view(g, t, pos):
        rows = span_of(pos, tok)
        return kb.at[g, rows, :] if t == 0 else vb.at[g, rows, pl.ds(0, HEAD_SIZE)]

    def kv_copy(g, t, src, dst, slot, target):
        return pltpu.make_async_remote_copy(
            src_ref=view(g, t, src),
            dst_ref=view(g, t, dst),
            send_sem=kv_send.at[g, t, slot],
            recv_sem=kv_recv.at[g, t, dst],
            device_id=target,
            device_id_type=MESH,
        )

    middle = (x == 1) | (x == 2)
    to_sib = [None] * 5
    plan = {
        0: [
            (0, x < NX - 1, 8, 6, x_up),
            (1, x == 0, 8, 2, x_dn),
            (2, None, 8, 0, nxt),
            (7, k == 0, 8, 7, sib),
        ],
        4: [
            (3, x >= 1, 0, 2, x_dn),
            (4, x == NX - 1, 0, 6, x_up),
            (7, k == 1, 0, 1, sib),
        ],
        1: [(6, middle, 6, 4, x_up), (8, None, 6, 5 + 2 * k, sib)],
        3: [(5, middle, 2, 4, x_dn), (9, None, 2, 1 + 2 * k, sib)],
        2: [(10, None, 4, 3 + 2 * k, sib)],
    }

    def kv_plan(g, t, s, act):
        for slot, cond, src, dst, target in plan[s]:
            c = kv_copy(g, t, src, dst, slot, target)
            if cond is None:
                act(c)
            else:

                @pl.when(cond)
                def _(c=c):
                    act(c)

    def kv_wait(g, t, pos):
        kv_copy(g, t, pos, pos, 0, sib).wait_recv()

    def kv_send_slot(g, t, s):
        if s:
            kv_wait(g, t, 8 - 2 * s)
        kv_plan(g, t, s, lambda c: c.start())

    def kv_rest(g):
        for t in range(2):
            for pos in (7, 5, 3, 1):
                kv_wait(g, t, pos)

    for c in kv_local:
        c.wait()
    for t in range(2):
        kv_send_slot(0, t, 0)

    for g in range(kv_heads):
        vb[g, :, pl.ds(HEAD_SIZE, HEAD_SIZE)] = jnp.ones((vb.shape[1], HEAD_SIZE), vb.dtype)
    base = i * blocks - SPAN * blocks
    lane = lax.broadcasted_iota(jnp.int32, (8, keys), 1) + first
    for j in range(blocks):
        block = base + lane // BLOCK
        keep = (block * BLOCK >= starts[j]) & (block <= i * blocks + j)
        bias[pl.ds(8 * j, 8), :] = jnp.where(keep, 0.0, MASKED)

    for t in range(2):
        for s in (4, 1):
            kv_send_slot(0, t, s)
    w_step(0)
    for t in range(2):
        for s in (3, 2):
            kv_send_slot(0, t, s)
    for t in range(2):
        kv_send_slot(1, t, 0)
    for c in q_local:
        c.wait()

    part = tok // 2

    def cols_of(n):
        return span_of(n, HEAD_SIZE)

    def h_copy(n, r):
        return pltpu.make_async_remote_copy(
            src_ref=ho.at[pl.ds(r * part, part), cols_of(n)],
            dst_ref=relay.at[r, :, cols_of(n)],
            send_sem=h_send.at[r, n],
            recv_sem=h_recv.at[r, n],
            device_id=(y_same, y_far)[r],
            device_id_type=MESH,
        )

    def f_copy(n, r):
        return pltpu.make_async_remote_copy(
            src_ref=relay.at[r, :, cols_of(n)],
            dst_ref=hin.at[pl.ds(r * part, part), cols_of(n)],
            send_sem=f_send.at[r, n],
            recv_sem=f_recv.at[r, n],
            device_id=(y_far, y_same)[r],
            device_id_type=MESH,
        )

    def forward(n):
        for r in range(2):
            h_copy(n, r).wait_recv()
            f_copy(n, r).start()

    tri = jnp.where(
        lax.broadcasted_iota(jnp.int32, (BLOCK, BLOCK), 1)
        <= lax.broadcasted_iota(jnp.int32, (BLOCK, BLOCK), 0),
        0.0,
        MASKED,
    )
    factor = HEAD_SIZE ** (-0.5) * math.log2(math.e)
    width = 2 * BLOCK
    chunks = keys // width
    own_first = SPAN * blocks - first // BLOCK

    def attend(n, g):
        q = qb[n]
        top = jnp.full((tok, BLOCK), MASKED, jnp.float32)
        for t in range(chunks):
            key = kb[g, pl.ds(first + t * width, width), :]
            s = lax.dot_general(q, key, (((1,), (1,)), ((), ())), preferred_element_type=jnp.float32)
            rows = []
            for j in range(blocks):
                lanes = []
                for u in range(2):
                    w = 2 * t + u
                    tile = s[j * BLOCK : (j + 1) * BLOCK, u * BLOCK : (u + 1) * BLOCK]
                    tile = tile + bias[pl.ds(8 * j, 1), pl.ds(w * BLOCK, BLOCK)]
                    if w == own_first + j:
                        tile = tile + tri
                    lanes.append(tile)
                rows.append(jnp.concatenate(lanes, axis=1))
            s = jnp.concatenate(rows, axis=0)
            sb[:, pl.ds(t * width, width)] = s
            top = jnp.maximum(top, jnp.maximum(s[:, :BLOCK], s[:, BLOCK:]))
        peak = jnp.max(top, axis=1, keepdims=True)
        for t in range(chunks):
            span = pl.ds(t * width, width)
            pb[:, span] = jnp.exp2((sb[:, span] - peak) * factor).astype(jnp.bfloat16)
        both = jnp.dot(pb[...], vb[g, pl.ds(first, keys), :], preferred_element_type=jnp.float32)
        out = both[:, :HEAD_SIZE] / both[:, HEAD_SIZE:]
        ho[:, cols_of(n)] = out.astype(jnp.bfloat16)
        for r in range(2):
            h_copy(n, r).start()

    tile_n = 512
    tiles = half // tile_n

    def project(src, wts, lo, hi, fresh):
        for m in range(tiles):
            cols = pl.ds(m * tile_n, tile_n)
            new = jnp.dot(src[:, lo:hi], wts[lo:hi, m * tile_n : (m + 1) * tile_n], preferred_element_type=jnp.float32)
            acc[:, cols] = new if fresh else acc[:, cols] + new

    kv_rest(0)

    def first_group(n, _):
        attend(n, 0)

        @pl.when(n == 0)
        def _():
            for t in range(2):
                for s in (4, 1):
                    kv_send_slot(1, t, s)
            w_step(1)

        @pl.when(n == 1)
        def _():
            for t in range(2):
                for s in (3, 2):
                    kv_send_slot(1, t, s)

        @pl.when(n > 0)
        def _():
            forward(n - 1)

        return 0

    lax.fori_loop(0, group, first_group, 0)
    w_step(2)
    kv_rest(1)

    def second_group(n, _):
        attend(n, 1)
        forward(n - 1)

        @pl.when(n == group + 1)
        def _():
            w_step(3)

        return 0

    lax.fori_loop(group, q_heads, second_group, 0)
    w_step(4)
    w_local.wait()
    mid = group * HEAD_SIZE
    full = q_heads * HEAD_SIZE
    forward(q_heads - 1)
    project(ho, wown, 0, full, True)
    for n in range(group):
        for r in range(2):
            f_copy(n, r).wait_recv()
    w_rest()
    project(hin, wfar, 0, mid, False)
    for n in range(group, q_heads):
        for r in range(2):
            f_copy(n, r).wait_recv()
    outs = []
    for m in range(tiles):
        cols = pl.ds(m * tile_n, tile_n)
        new = jnp.dot(hin[:, mid:], wfar[mid:, m * tile_n : (m + 1) * tile_n], preferred_element_type=jnp.float32)
        outb[:, cols] = (acc[:, cols] + new).astype(jnp.bfloat16)
        c = pltpu.make_async_copy(outb.at[:, cols], o_hbm.at[:, cols], out_sem.at[m])
        c.start()
        outs.append(c)

    w_first.wait_send()
    for d in w_plan:
        for p, sends in w_plan[d]:
            for slot, target in sends:
                w_copy(p, slot, target).wait_send()
    for g in range(kv_heads):
        for t in range(2):
            for s in plan:
                kv_plan(g, t, s, lambda c: c.wait_send())
    for n in range(q_heads):
        for r in range(2):
            h_copy(n, r).wait_send()
            f_copy(n, r).wait_send()
    for c in outs:
        c.wait()


def per_device(queries, keys, values, block_start, out_weight):
    n_ctx = lax.axis_size("ctx")
    tok = queries.shape[0]
    rows, width = out_weight.shape
    kv_heads = keys.shape[1] // HEAD_SIZE
    q_heads = queries.shape[1] // HEAD_SIZE
    half = width // 2
    nz = n_ctx // PLANE
    window = (SPAN + 1) * tok
    used = window - BLOCK
    bf16, f32 = jnp.bfloat16, jnp.float32
    dma = pltpu.SemaphoreType.DMA
    anywhere = pl.BlockSpec(memory_space=pl.ANY)
    return pl.pallas_call(
        kernel,
        out_shape=jax.ShapeDtypeStruct((tok, half), bf16),
        in_specs=[pl.BlockSpec(memory_space=pltpu.SMEM)] + [anywhere] * 4,
        out_specs=anywhere,
        scratch_shapes=[
            pltpu.VMEM((q_heads, tok, HEAD_SIZE), bf16),
            pltpu.VMEM((kv_heads, window, HEAD_SIZE), bf16),
            pltpu.VMEM((kv_heads, window, 2 * HEAD_SIZE), bf16),
            pltpu.VMEM((tok, used), f32),
            pltpu.VMEM((tok, used), bf16),
            pltpu.VMEM((8 * (tok // BLOCK), used), f32),
            pltpu.VMEM((tok, q_heads * HEAD_SIZE), bf16),
            pltpu.VMEM((tok, q_heads * HEAD_SIZE), bf16),
            pltpu.VMEM((2, tok // 2, q_heads * HEAD_SIZE), bf16),
            pltpu.VMEM((rows, half), bf16),
            pltpu.VMEM((rows, half), bf16),
            pltpu.VMEM((tok, half), f32),
            pltpu.VMEM((tok, half), bf16),
            dma((2 * kv_heads + q_heads + 1,)),
            dma((kv_heads, 2, 11)),
            dma((kv_heads, 2, SPAN + 1)),
            dma((4 * nz,)),
            dma((2 * nz,)),
            dma((2, q_heads)),
            dma((2, q_heads)),
            dma((2, q_heads)),
            dma((2, q_heads)),
            dma((half // 512,)),
        ],
        compiler_params=pltpu.CompilerParams(
            collective_id=0, has_side_effects=True, vmem_limit_bytes=56 * 1024 * 1024
        ),
    )(block_start, queries, keys, values, out_weight)


def solution(mesh):
    in_specs = (P("ctx", "head"), P("ctx", "head"), P("ctx", "head"), P("ctx"), P("head", None))
    out_specs = P("ctx", "head")
    return jax.shard_map(
        per_device, mesh=mesh, in_specs=in_specs, out_specs=out_specs, check_vma=False
    )
```

time: 201 us -> 71.4 us (0.36)
  the two profiles are of different devices: /device:TPU:1 before, /device:TPU:8 now
where the time goes in v1:
time: 71.4 us; the launch traced here: 71.3 us
  Pallas kernels  68.6 us (96%)
  local copies, waits for them, and re-layouts  2.73 us (4%)
    pallas_call x1, Pallas kernels, per_device(): pl.pallas_call(kernel, out_shape=jax.ShapeDtypeStruct((tok, half), bf16),...  68.6 us
    unnamed x1, local copies, waits for them, and re-layouts  2.73 us

profile of v1, /device:TPU:8, one launch (start us, length us, event | category | flops | bytes accessed | tf_op | source)
XLA Modules:
  0.0 71.3 jit_solution(6834911537842342643)
XLA Ops:
  0.0 68.6 %shard_map.55 = bf16[384,2048]{1,0:T(8,128)(2,1)} custom-call(s32[3]{0:T(128)} %starts.1, bf16[384,1024]{1,0:T(8,128)(2,1)} %q_hbm.1, bf16[384,256]{1,0:T(8,128)(2,1)} %k_hbm.1, bf16[384,256]{1,0:T(8,128)(2,1)} %v_hbm.1, bf16[1024,4096]{1,0:T(8,128)(2,1)} %w_hbm.1), custom_call_target="tpu_custom_call" | custom-call | tf_op jit(solution)/shard_map/pallas_call | solution.py:418
  68.6 2.7 %copy.7 = bf16[384,2048]{1,0:T(8,128)(2,1)} copy(bf16[384,2048]{1,0:T(8,128)(2,1)} %shard_map.55) | data formatting | bytes 3145728

commit v2 on v1

--- a/solution.py
+++ b/solution.py
@@ -38,7 +38,7 @@
     bias,
     ho,
     hin,
-    relay,
+    peaks,
     wown,
     wfar,
     acc,
@@ -50,8 +50,6 @@
     w_recv,
     h_send,
     h_recv,
-    f_send,
-    f_recv,
     out_sem,
 ):
     n_ctx = lax.axis_size("ctx")
@@ -61,7 +59,8 @@
     group = q_heads // kv_heads
     half = outb.shape[1]
     nz = n_ctx // PLANE
-    piece = wfar.shape[0] // (nz * 2)
+    cuts = 2
+    piece = wfar.shape[0] // (nz * 2 * cuts)
     up_hops = (nz - 1) // 2
     down_hops = nz - 1 - up_hops
     blocks = tok // BLOCK
@@ -85,8 +84,9 @@
     nxt = dev((i + ROW) % n_ctx, h)
     prv = dev((i + n_ctx - ROW) % n_ctx, h)
     yx = i + ROW - 2 * ROW * y_lo
-    y_same = dev(yx, h)
     y_far = dev(yx, 1 - h)
+    across = dev(i, 1 - h)
+    x_two = dev(row0 + ((x + 2) % NX) * 2, h)
     z_up = dev((i + PLANE) % n_ctx, h)
     z_dn = dev((i + n_ctx - PLANE) % n_ctx, h)
 
@@ -108,7 +108,7 @@
     w_local = load(w_hbm.at[:, span_of(h, half)], wown)
 
     barrier = pltpu.get_barrier_semaphore()
-    partners = (sib, x_up, x_dn, nxt, prv, y_far, z_up, z_dn)
+    partners = (sib, x_up, x_dn, x_two, nxt, prv, y_far, across, z_up, z_dn)
     for d in partners:
         pl.semaphore_signal(barrier, inc=1, device_id=d, device_id_type=MESH)
     pl.semaphore_wait(barrier, len(partners))
@@ -126,28 +126,32 @@
             device_id_type=MESH,
         )
 
-    mine = z * 2 + k
-    w_first = pltpu.make_async_remote_copy(
-        src_ref=w_hbm.at[w_rows(mine), span_of(1 - h, half)],
-        dst_ref=wfar.at[w_rows(mine), :],
-        send_sem=w_send.at[0],
-        recv_sem=w_recv.at[mine],
-        device_id=y_far,
-        device_id_type=MESH,
-    )
-    w_first.start()
-
-    w_plan = {0: [(mine, [(1, z_up), (2, z_dn), (3, sib)])]}
-    slots = 4
-    for d in range(1, down_hops + 1):
+    def w_first(c):
+        p = (z * 2 + k) * cuts + c
+        return pltpu.make_async_remote_copy(
+            src_ref=w_hbm.at[w_rows(p), span_of(1 - h, half)],
+            dst_ref=wfar.at[w_rows(p), :],
+            send_sem=w_send.at[c],
+            recv_sem=w_recv.at[p],
+            device_id=y_far,
+            device_id_type=MESH,
+        )
+
+    w_plan = {}
+    slots = cuts
+    for d in range(down_hops + 1):
         w_plan[d] = []
-        for reach, source, onward in (
-            (up_hops, (z + nz - d) % nz, z_up),
-            (down_hops, (z + d) % nz, z_dn),
-        ):
-            if d <= reach:
-                targets = [onward, sib] if d < reach else [sib]
-                w_plan[d].append((source * 2 + k, [(slots + n, c) for n, c in enumerate(targets)]))
+        for c in range(cuts):
+            up, down = (down_hops, up_hops) if c % 2 == 0 else (up_hops, down_hops)
+            routes = []
+            if d == 0:
+                routes.append((z, [z_up, z_dn, sib]))
+            elif d <= up:
+                routes.append(((z + nz - d) % nz, [z_up, sib] if d < up else [sib]))
+            if 0 < d <= down:
+                routes.append(((z + d) % nz, [z_dn, sib] if d < down else [sib]))
+            for source, targets in routes:
+                w_plan[d].append(((source * 2 + k) * cuts + c, [(slots + n, t) for n, t in enumerate(targets)]))
                 slots += len(targets)
 
     def w_step(d):
@@ -158,7 +162,8 @@
 
     def w_rest():
         for other in range(nz):
-            w_copy(other * 2 + 1 - k, 0, sib).wait_recv()
+            for c in range(cuts):
+                w_copy((other * 2 + 1 - k) * cuts + c, 0, sib).wait_recv()
 
     def view(g, t, pos):
         rows = span_of(pos, tok)
@@ -174,22 +179,23 @@
             device_id_type=MESH,
         )
 
-    middle = (x == 1) | (x == 2)
-    to_sib = [None] * 5
     plan = {
         0: [
-            (0, x < NX - 1, 8, 6, x_up),
-            (1, x == 0, 8, 2, x_dn),
-            (2, None, 8, 0, nxt),
-            (7, k == 0, 8, 7, sib),
+            (0, None, 8, 0, nxt),
+            (1, x <= 1, 8, 6, x_up),
+            (2, x == 0, 8, 4, x_two),
+            (3, x == 0, 8, 2, x_dn),
+            (4, k == 0, 8, 7, sib),
         ],
+        5: [(2, x == 1, 8, 4, x_two), (1, x == 2, 8, 6, x_up)],
         4: [
-            (3, x >= 1, 0, 2, x_dn),
-            (4, x == NX - 1, 0, 6, x_up),
-            (7, k == 1, 0, 1, sib),
+            (5, x >= 1, 0, 2, x_dn),
+            (6, x >= 2, 0, 4, x_two),
+            (7, x == NX - 1, 0, 6, x_up),
+            (4, k == 1, 0, 1, sib),
         ],
-        1: [(6, middle, 6, 4, x_up), (8, None, 6, 5 + 2 * k, sib)],
-        3: [(5, middle, 2, 4, x_dn), (9, None, 2, 1 + 2 * k, sib)],
+        1: [(8, None, 6, 5 + 2 * k, sib)],
+        3: [(9, None, 2, 1 + 2 * k, sib)],
         2: [(10, None, 4, 3 + 2 * k, sib)],
     }
 
@@ -208,19 +214,23 @@
         kv_copy(g, t, pos, pos, 0, sib).wait_recv()
 
     def kv_send_slot(g, t, s):
-        if s:
+        if 0 < s < 5:
             kv_wait(g, t, 8 - 2 * s)
         kv_plan(g, t, s, lambda c: c.start())
 
-    def kv_rest(g):
-        for t in range(2):
-            for pos in (7, 5, 3, 1):
-                kv_wait(g, t, pos)
+    def kv_rest(g, t):
+        for pos in (7, 5, 3, 1):
+            kv_wait(g, t, pos)
 
     for c in kv_local:
         c.wait()
     for t in range(2):
         kv_send_slot(0, t, 0)
+        kv_send_slot(0, t, 5)
+    for c in range(cuts):
+        w_first(c).start()
+    for t in range(2):
+        kv_send_slot(1, t, 0)
 
     for g in range(kv_heads):
         vb[g, :, pl.ds(HEAD_SIZE, HEAD_SIZE)] = jnp.ones((vb.shape[1], HEAD_SIZE), vb.dtype)
@@ -232,46 +242,29 @@
         bias[pl.ds(8 * j, 8), :] = jnp.where(keep, 0.0, MASKED)
 
     for t in range(2):
-        for s in (4, 1):
-            kv_send_slot(0, t, s)
+        kv_send_slot(0, t, 4)
+    for t in range(2):
+        kv_send_slot(1, t, 5)
     w_step(0)
     for t in range(2):
-        for s in (3, 2):
-            kv_send_slot(0, t, s)
-    for t in range(2):
-        kv_send_slot(1, t, 0)
+        kv_send_slot(1, t, 4)
+    for n in (1, 3, 2):
+        kv_send_slot(0, 0, n)
     for c in q_local:
         c.wait()
 
-    part = tok // 2
-
     def cols_of(n):
         return span_of(n, HEAD_SIZE)
 
-    def h_copy(n, r):
+    def h_copy(n):
         return pltpu.make_async_remote_copy(
-            src_ref=ho.at[pl.ds(r * part, part), cols_of(n)],
-            dst_ref=relay.at[r, :, cols_of(n)],
-            send_sem=h_send.at[r, n],
-            recv_sem=h_recv.at[r, n],
-            device_id=(y_same, y_far)[r],
+            src_ref=ho.at[:, cols_of(n)],
+            dst_ref=hin.at[:, cols_of(n)],
+            send_sem=h_send.at[n],
+            recv_sem=h_recv.at[n],
+            device_id=across,
             device_id_type=MESH,
         )
-
-    def f_copy(n, r):
-        return pltpu.make_async_remote_copy(
-            src_ref=relay.at[r, :, cols_of(n)],
-            dst_ref=hin.at[pl.ds(r * part, part), cols_of(n)],
-            send_sem=f_send.at[r, n],
-            recv_sem=f_recv.at[r, n],
-            device_id=(y_far, y_same)[r],
-            device_id_type=MESH,
-        )
-
-    def forward(n):
-        for r in range(2):
-            h_copy(n, r).wait_recv()
-            f_copy(n, r).start()
 
     tri = jnp.where(
         lax.broadcasted_iota(jnp.int32, (BLOCK, BLOCK), 1)
@@ -284,8 +277,8 @@
     chunks = keys // width
     own_first = SPAN * blocks - first // BLOCK
 
-    def attend(n, g):
-        q = qb[n]
+    def score(n, g):
+        q = qb[g * group + n]
         top = jnp.full((tok, BLOCK), MASKED, jnp.float32)
         for t in range(chunks):
             key = kb[g, pl.ds(first + t * width, width), :]
@@ -302,17 +295,19 @@
                     lanes.append(tile)
                 rows.append(jnp.concatenate(lanes, axis=1))
             s = jnp.concatenate(rows, axis=0)
-            sb[:, pl.ds(t * width, width)] = s
+            sb[n, :, pl.ds(t * width, width)] = s
             top = jnp.maximum(top, jnp.maximum(s[:, :BLOCK], s[:, BLOCK:]))
-        peak = jnp.max(top, axis=1, keepdims=True)
+        peaks[n] = top
+
+    def weigh(n, g):
+        peak = jnp.max(peaks[n], axis=1, keepdims=True)
         for t in range(chunks):
             span = pl.ds(t * width, width)
-            pb[:, span] = jnp.exp2((sb[:, span] - peak) * factor).astype(jnp.bfloat16)
+            pb[:, span] = jnp.exp2((sb[n, :, span] - peak) * factor).astype(jnp.bfloat16)
         both = jnp.dot(pb[...], vb[g, pl.ds(first, keys), :], preferred_element_type=jnp.float32)
         out = both[:, :HEAD_SIZE] / both[:, HEAD_SIZE:]
-        ho[:, cols_of(n)] = out.astype(jnp.bfloat16)
-        for r in range(2):
-            h_copy(n, r).start()
+        ho[:, cols_of(g * group + n)] = out.astype(jnp.bfloat16)
+        h_copy(g * group + n).start()
 
     tile_n = 512
     tiles = half // tile_n
@@ -323,69 +318,78 @@
             new = jnp.dot(src[:, lo:hi], wts[lo:hi, m * tile_n : (m + 1) * tile_n], preferred_element_type=jnp.float32)
             acc[:, cols] = new if fresh else acc[:, cols] + new
 
-    kv_rest(0)
-
-    def first_group(n, _):
-        attend(n, 0)
-
-        @pl.when(n == 0)
-        def _():
-            for t in range(2):
-                for s in (4, 1):
-                    kv_send_slot(1, t, s)
-            w_step(1)
-
-        @pl.when(n == 1)
-        def _():
-            for t in range(2):
-                for s in (3, 2):
-                    kv_send_slot(1, t, s)
-
-        @pl.when(n > 0)
-        def _():
-            forward(n - 1)
-
+    kv_rest(0, 0)
+
+    def hooks(g, n, table):
+        for (at_g, at_n), acts in table.items():
+
+            @pl.when((g == at_g) & (n == at_n))
+            def _(acts=acts):
+                for act in acts:
+                    act()
+
+    def slot(g, t, s):
+        return lambda: kv_send_slot(g, t, s)
+
+    after_score = {
+        (0, 1): [slot(0, 1, 1)],
+        (0, 2): [slot(0, 1, 3), lambda: w_step(1)],
+        (0, 3): [slot(0, 1, 2), lambda: kv_rest(0, 1)],
+        (1, 1): [slot(1, 1, 1)],
+        (1, 2): [slot(1, 1, 3)],
+        (1, 3): [slot(1, 1, 2), lambda: kv_rest(1, 1)],
+    }
+    after_weigh = {
+        (0, 1): [slot(1, 0, 1)],
+        (0, 2): [slot(1, 0, 3)],
+        (0, 3): [slot(1, 0, 2), lambda: w_step(2), lambda: kv_rest(1, 0)],
+        (1, 1): [lambda: w_step(3)],
+    }
+
+    def one_group(g, _):
+        def one_score(n, _):
+            score(n, g)
+            hooks(g, n, after_score)
+            return 0
+
+        def one_weigh(n, _):
+            weigh(n, g)
+            hooks(g, n, after_weigh)
+            return 0
+
+        lax.fori_loop(0, group, one_score, 0)
+        lax.fori_loop(0, group, one_weigh, 0)
         return 0
 
-    lax.fori_loop(0, group, first_group, 0)
-    w_step(2)
-    kv_rest(1)
-
-    def second_group(n, _):
-        attend(n, 1)
-        forward(n - 1)
-
-        @pl.when(n == group + 1)
-        def _():
-            w_step(3)
-
-        return 0
-
-    lax.fori_loop(group, q_heads, second_group, 0)
-    w_step(4)
+    lax.fori_loop(0, kv_heads, one_group, 0)
     w_local.wait()
     mid = group * HEAD_SIZE
+    late = (q_heads - 2) * HEAD_SIZE
     full = q_heads * HEAD_SIZE
-    forward(q_heads - 1)
     project(ho, wown, 0, full, True)
-    for n in range(group):
-        for r in range(2):
-            f_copy(n, r).wait_recv()
+    w_step(4)
+
+    def arrive(lo, hi):
+        for n in range(lo, hi):
+            h_copy(n).wait_recv()
+
     w_rest()
+    arrive(0, group)
     project(hin, wfar, 0, mid, False)
-    for n in range(group, q_heads):
-        for r in range(2):
-            f_copy(n, r).wait_recv()
+    arrive(group, q_heads - 2)
+    project(hin, wfar, mid, late, False)
+    arrive(q_heads - 2, q_heads)
     outs = []
     for m in range(tiles):
         cols = pl.ds(m * tile_n, tile_n)
-        new = jnp.dot(hin[:, mid:], wfar[mid:, m * tile_n : (m + 1) * tile_n], preferred_element_type=jnp.float32)
+        new = jnp.dot(hin[:, late:], wfar[late:, m * tile_n : (m + 1) * tile_n], preferred_element_type=jnp.float32)
         outb[:, cols] = (acc[:, cols] + new).astype(jnp.bfloat16)
         c = pltpu.make_async_copy(outb.at[:, cols], o_hbm.at[:, cols], out_sem.at[m])
         c.start()
         outs.append(c)
 
-    w_first.wait_send()
+    for c in range(cuts):
+        w_first(c).wait_send()
     for d in w_plan:
         for p, sends in w_plan[d]:
             for slot, target in sends:
@@ -395,9 +399,7 @@
             for s in plan:
                 kv_plan(g, t, s, lambda c: c.wait_send())
     for n in range(q_heads):
-        for r in range(2):
-            h_copy(n, r).wait_send()
-            f_copy(n, r).wait_send()
+        h_copy(n).wait_send()
     for c in outs:
         c.wait()
 
@@ -424,12 +426,12 @@
             pltpu.VMEM((q_heads, tok, HEAD_SIZE), bf16),
             pltpu.VMEM((kv_heads, window, HEAD_SIZE), bf16),
             pltpu.VMEM((kv_heads, window, 2 * HEAD_SIZE), bf16),
-            pltpu.VMEM((tok, used), f32),
+            pltpu.VMEM((q_heads // kv_heads, tok, used), f32),
             pltpu.VMEM((tok, used), bf16),
             pltpu.VMEM((8 * (tok // BLOCK), used), f32),
             pltpu.VMEM((tok, q_heads * HEAD_SIZE), bf16),
             pltpu.VMEM((tok, q_heads * HEAD_SIZE), bf16),
-            pltpu.VMEM((2, tok // 2, q_heads * HEAD_SIZE), bf16),
+            pltpu.VMEM((q_heads // kv_heads, tok, HEAD_SIZE), f32),
             pltpu.VMEM((rows, half), bf16),
             pltpu.VMEM((rows, half), bf16),
             pltpu.VMEM((tok, half), f32),
@@ -437,12 +439,10 @@
             dma((2 * kv_heads + q_heads + 1,)),
             dma((kv_heads, 2, 11)),
             dma((kv_heads, 2, SPAN + 1)),
+            dma((8 * nz,)),
             dma((4 * nz,)),
-            dma((2 * nz,)),
-            dma((2, q_heads)),
-            dma((2, q_heads)),
-            dma((2, q_heads)),
-            dma((2, q_heads)),
+            dma((q_heads,)),
+            dma((q_heads,)),
             dma((half // 512,)),
         ],
         compiler_params=pltpu.CompilerParams(

time: 71.4 us -> 60.2 us (0.84)
  the two profiles are of different devices: /device:TPU:8 before, /device:TPU:1 now
where the time goes in v2:
time: 60.2 us; the launch traced here: 60.1 us
  Pallas kernels  57.4 us (95%)
  local copies, waits for them, and re-layouts  2.73 us (5%)
    pallas_call x1, Pallas kernels, per_device(): pl.pallas_call(kernel, out_shape=jax.ShapeDtypeStruct((tok, half), bf16),...  57.4 us
    unnamed x1, local copies, waits for them, and re-layouts  2.73 us

profile of v2, /device:TPU:1, one launch (start us, length us, event | category | flops | bytes accessed | tf_op | source)
XLA Modules:
  0.0 60.1 jit_solution(3588979428604861729)
XLA Ops:
  0.0 57.4 %shard_map.55 = bf16[384,2048]{1,0:T(8,128)(2,1)} custom-call(s32[3]{0:T(128)} %starts.1, bf16[384,1024]{1,0:T(8,128)(2,1)} %q_hbm.1, bf16[384,256]{1,0:T(8,128)(2,1)} %k_hbm.1, bf16[384,256]{1,0:T(8,128)(2,1)} %v_hbm.1, bf16[1024,4096]{1,0:T(8,128)(2,1)} %w_hbm.1), custom_call_target="tpu_custom_call" | custom-call | tf_op jit(solution)/shard_map/pallas_call | solution.py:420
  57.4 2.7 %copy.7 = bf16[384,2048]{1,0:T(8,128)(2,1)} copy(bf16[384,2048]{1,0:T(8,128)(2,1)} %shard_map.55) | data formatting | bytes 3145728
